TPU v7x, 512 devices: a whole 4x4x16 slice. The times are simulated.
512 devices in a mesh: slab: 32 (over x, y, core), pencil: 16 (over z).
Axes of the slice: x: 4, y: 4, z: 16, core: 2. Of those that a mesh axis runs over, the one named last changes fastest.
Arguments:
- orbitals: float32 [4, 192, 192, 192], P(None, 'slab', 'pencil'), may hold values from -6 to 6
- potential: float32 [192, 192, 192], P('slab', 'pencil'), may hold values from 0.5 to 2.5
- unlocked: int32 [4], replicated, may hold values 0 or 1
Outputs:
- orthonormal: float32 [4, 192, 192, 192], P(None, 'slab', 'pencil')
Inputs may be any that keep to these rules, and one draw needn't show every extreme that they name: `unlocked`: 1 marks a band that is filtered, 0 a locked band kept as it is.
All inputs are finite; a program needn't handle non-finite values.
Results may differ from a plain program's by a relative error of at most 0.00005.
Values sent between devices are 32-bit elements; how exact they have to be, the bound alone decides.
No kernel may reach another device: no remote copies, remote signals or barrier semaphores. Data moves between devices by JAX's collectives and lax.ppermute only.
A program may use at most 64 MiB of HBM per device.

v0:
```python
import math
import jax
import jax.numpy as jnp
from jax import lax
from jax.sharding import PartitionSpec as P

NG = 192
kinetic_scale = 4.0
filter_center = 1.0
filter_half = 1.5
highest = lax.Precision.HIGHEST


def frequencies(number, length):
    index = jnp.arange(number, dtype=jnp.int32)
    return jnp.where(index < length // 2, index, index - length)


def tables(number, length):
    modes = frequencies(number, length)
    places = jnp.arange(length, dtype=jnp.int32)
    product = places[:, None] * modes[None, :] % length
    angle = 2.0 * math.pi / length * product.astype(jnp.float32)
    return (jnp.cos(angle), jnp.sin(angle))


def forward_table(cosine, sine):
    return jnp.stack([jnp.stack([cosine, -sine], 1), jnp.stack([sine, cosine], 1)], 1)


def inverse_table(cosine, sine):
    cos_t = cosine.T
    sin_t = sine.T
    return jnp.stack([jnp.stack([cos_t, sin_t], 1), jnp.stack([-sin_t, cos_t], 1)], 1)


def local(orbitals, potential, unlocked):
    length = orbitals.shape[3]
    cos_k, sin_k = tables(length, length)
    cos_f, sin_f = tables(length, length)
    first_forward = jnp.stack([cos_k, -sin_k], 1)
    first_inverse = jnp.stack([cos_k.T, -sin_k.T], 1)
    second_forward = forward_table(cos_k, sin_k)
    second_inverse = inverse_table(cos_k, sin_k)
    depth_forward = forward_table(cos_f, sin_f)
    depth_inverse = inverse_table(cos_f, sin_f)
    pencil_block = length // lax.axis_size("pencil")
    slab_block = length // lax.axis_size("slab")
    kept_list = frequencies(length, length)
    third_modes = lax.dynamic_slice_in_dim(
        kept_list, lax.axis_index("pencil") * pencil_block, pencil_block
    ).astype(jnp.float32)
    second_modes = lax.dynamic_slice_in_dim(
        kept_list, lax.axis_index("slab") * slab_block, slab_block
    ).astype(jnp.float32)
    first_modes = frequencies(length, length).astype(jnp.float32)
    squared = (
        third_modes[:, None, None] ** 2
        + second_modes[None, :, None] ** 2
        + first_modes[None, None, :] ** 2
    )
    radius = float((length // 4) ** 2)
    kinetic = jnp.where(squared < radius, kinetic_scale * squared / radius, 0.0)
    lines_k = jnp.einsum("bacx,xrk->bacrk", orbitals, first_forward, precision=highest)
    along_f = jnp.einsum(
        "bacrk,crsf->baksf",
        lax.all_to_all(lines_k, "pencil", split_axis=4, concat_axis=2, tiled=True),
        second_forward,
        precision=highest,
    )
    spectra = jnp.einsum(
        "baksf,astg->bkftg",
        lax.all_to_all(along_f, "slab", split_axis=4, concat_axis=1, tiled=True),
        depth_forward,
        precision=highest,
    )
    spectra = spectra * kinetic[None, :, :, None, :]
    along_a = jnp.einsum("bkftg,gtsa->bkfsa", spectra, depth_inverse, precision=highest)
    returned = lax.all_to_all(along_a, "slab", split_axis=4, concat_axis=2, tiled=True)
    rows_c = jnp.einsum("bkfsa,fsrc->bkarc", returned, second_inverse, precision=highest)
    lines_x = lax.all_to_all(rows_c, "pencil", split_axis=4, concat_axis=1, tiled=True)
    kinetic_part = jnp.einsum("bkarc,krx->bacx", lines_x, first_inverse, precision=highest)
    kinetic_part = kinetic_part / float(NG**3)
    applied = kinetic_part + potential[None] * orbitals
    filtered = jnp.where(
        unlocked[:, None, None, None] == 1,
        (applied - filter_center * orbitals) / filter_half,
        orbitals,
    )
    number = filtered.shape[0]
    flattened = filtered.reshape(number, -1)
    partial_intersection = jnp.dot(flattened, flattened.T, precision=highest) / float(NG**3)
    intersection = lax.psum(partial_intersection, ("slab", "pencil"))
    factor = jnp.linalg.cholesky(intersection)
    result = jax.scipy.linalg.solve_triangular(factor, flattened, lower=True)
    return result.reshape(filtered.shape)


def solution(mesh):
    in_specs = (P(None, "slab", "pencil", None), P("slab", "pencil", None), P())
    out_specs = P(None, "slab", "pencil", None)
    return jax.shard_map(local, mesh=mesh, in_specs=in_specs, out_specs=out_specs, check_vma=False)
```

profile of v0, /device:TPU:1, one launch (start us, length us, event | category | flops | bytes accessed | tf_op | source)
XLA Modules:
  0.0 365.7 jit_solution(14531609065697997235)
XLA Ops:
  3.5 3.5 copy.74
  7.0 7.7 %reshape.301 = f32[16,1,6912]{2,1,0:T(1,128)} reshape(f32[192,6,2,4,12]{4,3,2,1,0:T(4,128)} %bitcast.136) | data formatting | bytes 884736
  14.7 15.9 %all-to-all-start = ((f32[16,1,6912]{2,1,0:T(1,128)}), f32[16,1,6912]{2,1,0:T(1,128)S(1)}, u32[]{:S(2)}, u32[]{:S(2)}) async-start(f32[16,1,6912]{2,1,0:T(1,128)} %reshape.301), calls=%async_computation | async-start | bytes 884736 | tf_op jit(solution)/shard_map/all_to_all | solution.py:67
  30.9 20.2 %all-to-all-done = f32[16,1,6912]{2,1,0:T(1,128)S(1)} async-done(((f32[16,1,6912]{2,1,0:T(1,128)}), f32[16,1,6912]{2,1,0:T(1,128)S(1)}, u32[]{:S(2)}, u32[]{:S(2)}) %all-to-all-start) | async-done | bytes 442400 | tf_op jit(solution)/shard_map/all_to_all | solution.py:67
  53.3 7.8 %reshape.302 = f32[192,6,2,4,12]{4,3,2,1,0:T(4,128)} reshape(f32[16,6912]{1,0:T(8,128)S(1)} %reduce.6) | data formatting | bytes 884736
  61.0 7.2 %copy.163 = f32[4,6,12,2,16,12]{2,4,3,5,1,0:T(8,128)} copy(f32[4,6,12,2,16,12]{2,0,3,1,5,4:T(4,128)} %bitcast.137) | data formatting | bytes 884736 | tf_op jit(solution)/shard_map/all_to_all | solution.py:67
  68.3 4.3 %all_to_all.55 = f32[4,6,192,2,12]{2,3,4,1,0:T(2,128)S(1)} reshape(f32[4,6,16,12,2,12]{3,2,4,5,1,0:T(8,128)} %bitcast.138) | data formatting | bytes 884736 | tf_op jit(solution)/shard_map/all_to_all | solution.py:67
  74.1 4.8 %copy.79 = f32[4,6,12,2,192]{2,3,1,0,4:T(2,128)} copy(f32[4,6,12,2,192]{4,2,3,1,0:T(8,128)S(1)} %convolution_bitcast_fusion.3) | data formatting | bytes 884736 | tf_op jit(solution)/shard_map/bacrk,crsf->baksf/dot_general | solution.py:65
  78.9 8.6 %reshape.303 = f32[32,1,3456]{2,1,0:T(1,128)} reshape(f32[192,4,6,2,12]{4,3,2,1,0:T(2,128)} %bitcast.139) | data formatting | bytes 884736
  87.5 14.1 %all-to-all-start.1 = ((f32[32,1,3456]{2,1,0:T(1,128)}), f32[32,1,3456]{2,1,0:T(1,128)S(1)}, u32[]{:S(2)}, u32[]{:S(2)}) async-start(f32[32,1,3456]{2,1,0:T(1,128)} %reshape.303), calls=%async_computation.1 | async-start | bytes 884736 | tf_op jit(solution)/shard_map/all_to_all | solution.py:73
  101.7 10.5 %all-to-all-done.1 = f32[32,1,3456]{2,1,0:T(1,128)S(1)} async-done(((f32[32,1,3456]{2,1,0:T(1,128)}), f32[32,1,3456]{2,1,0:T(1,128)S(1)}, u32[]{:S(2)}, u32[]{:S(2)}) %all-to-all-start.1) | async-done | bytes 442400 | tf_op jit(solution)/shard_map/all_to_all | solution.py:73
  113.9 8.9 %reshape.304 = f32[192,4,6,2,12]{4,3,2,1,0:T(2,128)} reshape(f32[32,3456]{1,0:T(8,128)S(1)} %reduce.7) | data formatting | bytes 884736
  122.9 6.1 %copy.81 = f32[4,32,6,12,2,6]{3,4,5,2,1,0:T(2,128)} copy(f32[4,32,6,12,2,6]{3,4,2,0,5,1:T(2,128)} %bitcast.140) | data formatting | bytes 884736 | tf_op jit(solution)/shard_map/all_to_all | solution.py:73
  129.0 6.3 %copy.107 = f32[4,192,12,2,6,1]{1,4,3,5,2,0:T(8,128)S(1)} copy(f32[4,192,12,2,6,1]{2,3,4,1,0,5:T(2,128)} %bitcast.141) | data formatting | bytes 884736 | tf_op jit(solution)/shard_map/all_to_all | solution.py:73
  135.3 3.0 fusion.1
  138.3 3.0 convolution_bitcast_fusion
  141.3 3.7 %copy.85 = f32[4,12,6,2,192]{1,0,3,2,4:T(4,128)} copy(f32[4,12,6,2,192]{4,2,3,1,0:T(8,128)S(1)} %convolution_bitcast_fusion) | data formatting | bytes 884736 | tf_op jit(solution)/shard_map/bkftg,gtsa->bkfsa/dot_general | solution.py:78
  145.0 7.2 %reshape.305 = f32[32,1,3456]{2,1,0:T(1,128)S(1)} reshape(f32[192,6,2,4,12]{4,3,2,1,0:T(4,128)} %bitcast.142) | data formatting | bytes 884736
  152.2 14.1 %all_to_all.72 = f32[32,1,3456]{2,1,0:T(1,128)S(1)} all-to-all(f32[32,1,3456]{2,1,0:T(1,128)S(1)} %reshape.305), channel_id=1, replica_groups=mesh['slab'=32,'pencil'=16] {'slab'}, dimensions={0} | all-to-all | bytes 884736 | tf_op jit(solution)/shard_map/all_to_all | solution.py:79
  168.1 7.8 %reshape.306 = f32[192,6,2,4,12]{4,3,2,1,0:T(4,128)} reshape(f32[32,3456]{1,0:T(8,128)S(1)} %reduce.8) | data formatting | bytes 884736
  175.8 4.8 %copy.86 = f32[4,12,6,2,192]{1,3,4,2,0:T(2,128)S(1)} copy(f32[4,12,6,2,192]{1,0,3,2,4:T(4,128)} %bitcast.143) | data formatting | bytes 884736 | tf_op jit(solution)/shard_map/all_to_all | solution.py:79
  180.6 3.7 %copy.87 = f32[4,12,32,6,2,6]{1,4,5,3,2,0:T(2,128)} copy(f32[4,12,32,6,2,6]{1,4,5,2,3,0:T(2,128)S(1)} %bitcast.144) | data formatting | bytes 884736 | tf_op jit(solution)/shard_map/all_to_all | solution.py:79
  184.3 6.3 %copy.113 = f32[4,12,192,2,6,1]{2,4,3,5,1,0:T(8,128)S(1)} copy(f32[4,12,192,2,6,1]{1,3,4,2,0,5:T(2,128)} %bitcast.145) | data formatting | bytes 884736 | tf_op jit(solution)/shard_map/all_to_all | solution.py:79
  190.6 3.0 convolution_bitcast_fusion.1
  193.6 3.7 %copy.90 = f32[4,12,6,2,192]{1,0,3,2,4:T(4,128)} copy(f32[4,12,6,2,192]{4,2,3,1,0:T(8,128)S(1)} %convolution_bitcast_fusion.1) | data formatting | bytes 884736 | tf_op jit(solution)/shard_map/bkfsa,fsrc->bkarc/dot_general | solution.py:80
  197.4 7.9 %reshape.307 = f32[16,1,6912]{2,1,0:T(1,128)} reshape(f32[192,6,2,4,12]{4,3,2,1,0:T(4,128)} %bitcast.146) | data formatting | bytes 884736
  205.3 5.6 %all-to-all-start.3 = ((f32[16,1,6912]{2,1,0:T(1,128)}), f32[16,1,6912]{2,1,0:T(1,128)S(1)}, u32[]{:S(2)}, u32[]{:S(2)}) async-start(f32[16,1,6912]{2,1,0:T(1,128)} %reshape.307), calls=%async_computation.3 | async-start | bytes 884736 | tf_op jit(solution)/shard_map/all_to_all | solution.py:81
  210.9 21.6 %all-to-all-done.3 = f32[16,1,6912]{2,1,0:T(1,128)S(1)} async-done(((f32[16,1,6912]{2,1,0:T(1,128)}), f32[16,1,6912]{2,1,0:T(1,128)S(1)}, u32[]{:S(2)}, u32[]{:S(2)}) %all-to-all-start.3) | async-done | bytes 442400 | tf_op jit(solution)/shard_map/all_to_all | solution.py:81
  234.2 7.8 %reshape.308 = f32[192,6,2,4,12]{4,3,2,1,0:T(4,128)} reshape(f32[16,6912]{1,0:T(8,128)S(1)} %reduce.9) | data formatting | bytes 884736
  242.0 7.2 %copy.162 = f32[4,12,6,2,16,12]{1,4,3,5,2,0:T(8,128)} copy(f32[4,12,6,2,16,12]{1,0,3,2,5,4:T(4,128)} %bitcast.147) | data formatting | bytes 884736 | tf_op jit(solution)/shard_map/all_to_all | solution.py:81
  249.2 4.4 %all_to_all.67 = f32[4,192,6,2,12]{1,3,4,2,0:T(2,128)S(1)} reshape(f32[4,16,12,6,2,12]{2,1,4,5,3,0:T(8,128)} %bitcast.148) | data formatting | bytes 884736 | tf_op jit(solution)/shard_map/all_to_all | solution.py:81
  256.1 105.4 %psum.7 = f32[4,4]{0,1:T(4,128)S(1)} all-reduce(f32[4,4]{0,1:T(4,128)S(1)} %fusion.7), channel_id=1, replica_groups=mesh['slab'=32,'pencil'=16] {'slab','pencil'}, use_global_device_ids=true, to_apply=%region_0.1 | all-reduce | flops 16 | bytes 128 | tf_op jit(solution)/shard_map/psum | solution.py:93
  (34 shorter events, 19.0 us)
Async XLA Ops:
  14.7 36.4 %all-to-all-start = ((f32[16,1,6912]{2,1,0:T(1,128)}), f32[16,1,6912]{2,1,0:T(1,128)S(1)}, u32[]{:S(2)}, u32[]{:S(2)}) async-start(f32[16,1,6912]{2,1,0:T(1,128)} %reshape.301), calls=%async_computation | async-start | bytes 884736 | tf_op jit(solution)/shard_map/all_to_all | solution.py:67
  87.5 24.7 %all-to-all-start.1 = ((f32[32,1,3456]{2,1,0:T(1,128)}), f32[32,1,3456]{2,1,0:T(1,128)S(1)}, u32[]{:S(2)}, u32[]{:S(2)}) async-start(f32[32,1,3456]{2,1,0:T(1,128)} %reshape.303), calls=%async_computation.1 | async-start | bytes 884736 | tf_op jit(solution)/shard_map/all_to_all | solution.py:73
  193.6 17.3 %copy-start.2 = (s32[4]{0:T(128)S(1)}, s32[4]{0:T(128)}, u32[]{:S(2)}) copy-start(s32[4]{0:T(128)} %param.5) | copy-start | bytes 52
  205.3 27.3 %all-to-all-start.3 = ((f32[16,1,6912]{2,1,0:T(1,128)}), f32[16,1,6912]{2,1,0:T(1,128)S(1)}, u32[]{:S(2)}, u32[]{:S(2)}) async-start(f32[16,1,6912]{2,1,0:T(1,128)} %reshape.307), calls=%async_computation.3 | async-start | bytes 884736 | tf_op jit(solution)/shard_map/all_to_all | solution.py:81
  249.2 4.4 %copy-start = (f32[4,6,12,192]{3,0,2,1:T(4,128)S(1)}, f32[4,6,12,192]{3,0,2,1:T(4,128)}, u32[]{:S(2)}) copy-start(f32[4,6,12,192]{3,0,2,1:T(4,128)} %param.3) | copy-start | bytes 663556
  249.2 4.4 %copy-start.1 = (f32[6,12,192]{2,1,0:T(8,128)S(1)}, f32[6,12,192]{2,1,0:T(8,128)}, u32[]{:S(2)}) copy-start(f32[6,12,192]{2,1,0:T(8,128)} %param.4) | copy-start | bytes 165892
where the time goes:
time: 371 us; the launch traced here: 366 us
  local copies, waits for them, and re-layouts  131 us (35%)
  blocking collectives  120 us (32%)
  waiting for transfers between devices  52.3 us (14%)
  starting transfers between devices  35.6 us (10%)
  matrix products  16.2 us (4%)
  other arithmetic  10.9 us (3%)
    psum x1, blocking collectives, local(): intersection = lax.psum(partial_intersection, ('slab', 'pencil'))  105 us
    unnamed x14, local copies, waits for them, and re-layouts  63.6 us
    all_to_all x1, waiting for transfers between devices, local(): lax.all_to_all(rows_c, 'pencil', split_axis=4, concat_axis=1, tiled=True)  21.6 us
    all_to_all x1, waiting for transfers between devices, local(): lax.all_to_all(lines_k, 'pencil', split_axis=4, concat_axis=2, tiled=True)  20.2 us
    all_to_all x1, starting transfers between devices, local(): lax.all_to_all(lines_k, 'pencil', split_axis=4, concat_axis=2, tiled=True)  15.9 us
    all_to_all x3, local copies, waits for them, and re-layouts, local(): lax.all_to_all(along_a, 'slab', split_axis=4, concat_axis=2, tiled=True)  14.8 us
    all_to_all x1, blocking collectives, local(): lax.all_to_all(along_a, 'slab', split_axis=4, concat_axis=2, tiled=True)  14.1 us
    all_to_all x1, starting transfers between devices, local(): lax.all_to_all(along_f, 'slab', split_axis=4, concat_axis=1, tiled=True)  14.1 us
  transfers between devices with their start and end apart: 3, of which 3 were waited for; matrix products, arithmetic and copies ran while one was open for 0% of the time, Pallas kernels for 0%

commit v1 on v0

--- a/solution.py
+++ b/solution.py
@@ -90,7 +90,7 @@
     number = filtered.shape[0]
     flattened = filtered.reshape(number, -1)
     partial_intersection = jnp.dot(flattened, flattened.T, precision=highest) / float(NG**3)
-    intersection = lax.psum(partial_intersection, ("slab", "pencil"))
+    intersection = jnp.sum(lax.all_gather(partial_intersection, ("slab", "pencil")), axis=0)
     factor = jnp.linalg.cholesky(intersection)
     result = jax.scipy.linalg.solve_triangular(factor, flattened, lower=True)
     return result.reshape(filtered.shape)

time: 371 us -> 407 us (1.097)
  the two profiles are of different devices: /device:TPU:1 before, /device:TPU:2 now
where the time goes in v1:
time: 407 us; the launch traced here: 401 us
  blocking collectives  151 us (37%)
  local copies, waits for them, and re-layouts  131 us (32%)
  waiting for transfers between devices  61.7 us (15%)
  starting transfers between devices  29.5 us (7%)
  matrix products  16.2 us (4%)
  other arithmetic  11.5 us (3%)
    all_gather x1, blocking collectives, local(): lax.all_gather(partial_intersection, ('slab', 'pencil'))  137 us
    unnamed x14, local copies, waits for them, and re-layouts  63.6 us
    all_to_all x1, waiting for transfers between devices, local(): lax.all_to_all(rows_c, 'pencil', split_axis=4, concat_axis=1, tiled=True)  27.1 us
    all_to_all x1, waiting for transfers between devices, local(): lax.all_to_all(lines_k, 'pencil', split_axis=4, concat_axis=2, tiled=True)  25.7 us
    all_to_all x1, starting transfers between devices, local(): lax.all_to_all(lines_k, 'pencil', split_axis=4, concat_axis=2, tiled=True)  15.4 us
    all_to_all x3, local copies, waits for them, and re-layouts, local(): lax.all_to_all(along_a, 'slab', split_axis=4, concat_axis=2, tiled=True)  14.8 us
    all_to_all x1, blocking collectives, local(): lax.all_to_all(along_a, 'slab', split_axis=4, concat_axis=2, tiled=True)  14.1 us
    all_to_all x2, local copies, waits for them, and re-layouts, local(): lax.all_to_all(along_f, 'slab', split_axis=4, concat_axis=1, tiled=True)  12.4 us
  transfers between devices with their start and end apart: 3, of which 3 were waited for; matrix products, arithmetic and copies ran while one was open for 0% of the time, Pallas kernels for 0%

profile of v1, /device:TPU:2, one launch (start us, length us, event | category | flops | bytes accessed | tf_op | source)
XLA Modules:
  0.0 401.4 jit_solution(13529341976312542950)
XLA Ops:
  3.5 3.5 copy.71
  7.0 7.7 %reshape.305 = f32[16,1,6912]{2,1,0:T(1,128)} reshape(f32[192,6,2,4,12]{4,3,2,1,0:T(4,128)} %bitcast.142) | data formatting | bytes 884736
  14.7 15.4 %all-to-all-start = ((f32[16,1,6912]{2,1,0:T(1,128)}), f32[16,1,6912]{2,1,0:T(1,128)S(1)}, u32[]{:S(2)}, u32[]{:S(2)}) async-start(f32[16,1,6912]{2,1,0:T(1,128)} %reshape.305), calls=%async_computation | async-start | bytes 884736 | tf_op jit(solution)/shard_map/all_to_all | solution.py:67
  30.4 25.7 %all-to-all-done = f32[16,1,6912]{2,1,0:T(1,128)S(1)} async-done(((f32[16,1,6912]{2,1,0:T(1,128)}), f32[16,1,6912]{2,1,0:T(1,128)S(1)}, u32[]{:S(2)}, u32[]{:S(2)}) %all-to-all-start) | async-done | bytes 442400 | tf_op jit(solution)/shard_map/all_to_all | solution.py:67
  58.3 7.8 %reshape.306 = f32[192,6,2,4,12]{4,3,2,1,0:T(4,128)} reshape(f32[16,6912]{1,0:T(8,128)S(1)} %reduce.7) | data formatting | bytes 884736
  66.1 7.2 %copy.158 = f32[4,6,12,2,16,12]{2,4,3,5,1,0:T(8,128)} copy(f32[4,6,12,2,16,12]{2,0,3,1,5,4:T(4,128)} %bitcast.143) | data formatting | bytes 884736 | tf_op jit(solution)/shard_map/all_to_all | solution.py:67
  73.3 4.3 %all_to_all.55 = f32[4,6,192,2,12]{2,3,4,1,0:T(2,128)S(1)} reshape(f32[4,6,16,12,2,12]{3,2,4,5,1,0:T(8,128)} %bitcast.144) | data formatting | bytes 884736 | tf_op jit(solution)/shard_map/all_to_all | solution.py:67
  79.1 4.8 %copy.76 = f32[4,6,12,2,192]{2,3,1,0,4:T(2,128)} copy(f32[4,6,12,2,192]{4,2,3,1,0:T(8,128)S(1)} %convolution_bitcast_fusion.3) | data formatting | bytes 884736 | tf_op jit(solution)/shard_map/bacrk,crsf->baksf/dot_general | solution.py:65
  84.0 8.6 %reshape.307 = f32[32,1,3456]{2,1,0:T(1,128)} reshape(f32[192,4,6,2,12]{4,3,2,1,0:T(2,128)} %bitcast.145) | data formatting | bytes 884736
  92.5 8.2 %all-to-all-start.1 = ((f32[32,1,3456]{2,1,0:T(1,128)}), f32[32,1,3456]{2,1,0:T(1,128)S(1)}, u32[]{:S(2)}, u32[]{:S(2)}) async-start(f32[32,1,3456]{2,1,0:T(1,128)} %reshape.307), calls=%async_computation.1 | async-start | bytes 884736 | tf_op jit(solution)/shard_map/all_to_all | solution.py:73
  100.9 8.9 %all-to-all-done.1 = f32[32,1,3456]{2,1,0:T(1,128)S(1)} async-done(((f32[32,1,3456]{2,1,0:T(1,128)}), f32[32,1,3456]{2,1,0:T(1,128)S(1)}, u32[]{:S(2)}, u32[]{:S(2)}) %all-to-all-start.1) | async-done | bytes 442400 | tf_op jit(solution)/shard_map/all_to_all | solution.py:73
  111.5 8.9 %reshape.308 = f32[192,4,6,2,12]{4,3,2,1,0:T(2,128)} reshape(f32[32,3456]{1,0:T(8,128)S(1)} %reduce.8) | data formatting | bytes 884736
  120.4 6.1 %copy.78 = f32[4,32,6,12,2,6]{3,4,5,2,1,0:T(2,128)} copy(f32[4,32,6,12,2,6]{3,4,2,0,5,1:T(2,128)} %bitcast.146) | data formatting | bytes 884736 | tf_op jit(solution)/shard_map/all_to_all | solution.py:73
  126.5 6.3 %copy.103 = f32[4,192,12,2,6,1]{1,4,3,5,2,0:T(8,128)S(1)} copy(f32[4,192,12,2,6,1]{2,3,4,1,0,5:T(2,128)} %bitcast.147) | data formatting | bytes 884736 | tf_op jit(solution)/shard_map/all_to_all | solution.py:73
  132.8 3.0 fusion.1
  135.8 3.0 convolution_bitcast_fusion
  138.8 3.7 copy.82
  142.6 7.2 %reshape.309 = f32[32,1,3456]{2,1,0:T(1,128)S(1)} reshape(f32[192,6,2,4,12]{4,3,2,1,0:T(4,128)} %bitcast.148) | data formatting | bytes 884736
  149.8 14.1 %all_to_all.72 = f32[32,1,3456]{2,1,0:T(1,128)S(1)} all-to-all(f32[32,1,3456]{2,1,0:T(1,128)S(1)} %reshape.309), channel_id=1, replica_groups=mesh['slab'=32,'pencil'=16] {'slab'}, dimensions={0} | all-to-all | bytes 884736 | tf_op jit(solution)/shard_map/all_to_all | solution.py:79
  165.6 7.8 %reshape.310 = f32[192,6,2,4,12]{4,3,2,1,0:T(4,128)} reshape(f32[32,3456]{1,0:T(8,128)S(1)} %reduce.9) | data formatting | bytes 884736
  173.3 4.8 %copy.83 = f32[4,12,6,2,192]{1,3,4,2,0:T(2,128)S(1)} copy(f32[4,12,6,2,192]{1,0,3,2,4:T(4,128)} %bitcast.149) | data formatting | bytes 884736 | tf_op jit(solution)/shard_map/all_to_all | solution.py:79
  178.1 3.7 copy.84
  181.8 6.3 %copy.109 = f32[4,12,192,2,6,1]{2,4,3,5,1,0:T(8,128)S(1)} copy(f32[4,12,192,2,6,1]{1,3,4,2,0,5:T(2,128)} %bitcast.151) | data formatting | bytes 884736 | tf_op jit(solution)/shard_map/all_to_all | solution.py:79
  188.1 3.0 convolution_bitcast_fusion.1
  191.2 3.7 copy.87
  194.9 7.9 %reshape.311 = f32[16,1,6912]{2,1,0:T(1,128)} reshape(f32[192,6,2,4,12]{4,3,2,1,0:T(4,128)} %bitcast.152) | data formatting | bytes 884736
  202.8 5.9 %all-to-all-start.3 = ((f32[16,1,6912]{2,1,0:T(1,128)}), f32[16,1,6912]{2,1,0:T(1,128)S(1)}, u32[]{:S(2)}, u32[]{:S(2)}) async-start(f32[16,1,6912]{2,1,0:T(1,128)} %reshape.311), calls=%async_computation.3 | async-start | bytes 884736 | tf_op jit(solution)/shard_map/all_to_all | solution.py:81
  208.7 27.1 %all-to-all-done.3 = f32[16,1,6912]{2,1,0:T(1,128)S(1)} async-done(((f32[16,1,6912]{2,1,0:T(1,128)}), f32[16,1,6912]{2,1,0:T(1,128)S(1)}, u32[]{:S(2)}, u32[]{:S(2)}) %all-to-all-start.3) | async-done | bytes 442400 | tf_op jit(solution)/shard_map/all_to_all | solution.py:81
  237.5 7.8 %reshape.312 = f32[192,6,2,4,12]{4,3,2,1,0:T(4,128)} reshape(f32[16,6912]{1,0:T(8,128)S(1)} %reduce.10) | data formatting | bytes 884736
  245.3 7.2 %copy.157 = f32[4,12,6,2,16,12]{1,4,3,5,2,0:T(8,128)} copy(f32[4,12,6,2,16,12]{1,0,3,2,5,4:T(4,128)} %bitcast.153) | data formatting | bytes 884736 | tf_op jit(solution)/shard_map/all_to_all | solution.py:81
  252.5 4.4 %all_to_all.67 = f32[4,192,6,2,12]{1,3,4,2,0:T(2,128)S(1)} reshape(f32[4,16,12,6,2,12]{2,1,4,5,3,0:T(8,128)} %bitcast.154) | data formatting | bytes 884736 | tf_op jit(solution)/shard_map/all_to_all | solution.py:81
  259.5 137.0 %all-gather.1 = f32[512,4,4]{2,1,0:T(4,128)S(1)} all-gather(f32[1,4,4]{2,1,0:T(4,128)S(1)} %fusion.8), channel_id=2, replica_groups=mesh['slab'=32,'pencil'=16] {'slab','pencil'}, dimensions={0}, use_global_device_ids=true | all-gather | bytes 32832 | tf_op jit(solution)/shard_map/all_gather | solution.py:93
  (35 shorter events, 19.6 us)
Async XLA Ops:
  14.7 41.4 %all-to-all-start = ((f32[16,1,6912]{2,1,0:T(1,128)}), f32[16,1,6912]{2,1,0:T(1,128)S(1)}, u32[]{:S(2)}, u32[]{:S(2)}) async-start(f32[16,1,6912]{2,1,0:T(1,128)} %reshape.305), calls=%async_computation | async-start | bytes 884736 | tf_op jit(solution)/shard_map/all_to_all | solution.py:67
  92.5 17.2 %all-to-all-start.1 = ((f32[32,1,3456]{2,1,0:T(1,128)}), f32[32,1,3456]{2,1,0:T(1,128)S(1)}, u32[]{:S(2)}, u32[]{:S(2)}) async-start(f32[32,1,3456]{2,1,0:T(1,128)} %reshape.307), calls=%async_computation.1 | async-start | bytes 884736 | tf_op jit(solution)/shard_map/all_to_all | solution.py:73
  191.1 17.5 %copy-start.2 = (s32[4]{0:T(128)S(1)}, s32[4]{0:T(128)}, u32[]{:S(2)}) copy-start(s32[4]{0:T(128)} %param.5) | copy-start | bytes 52
  202.8 33.0 %all-to-all-start.3 = ((f32[16,1,6912]{2,1,0:T(1,128)}), f32[16,1,6912]{2,1,0:T(1,128)S(1)}, u32[]{:S(2)}, u32[]{:S(2)}) async-start(f32[16,1,6912]{2,1,0:T(1,128)} %reshape.311), calls=%async_computation.3 | async-start | bytes 884736 | tf_op jit(solution)/shard_map/all_to_all | solution.py:81
  252.5 4.4 %copy-start = (f32[4,6,12,192]{3,0,2,1:T(4,128)S(1)}, f32[4,6,12,192]{3,0,2,1:T(4,128)}, u32[]{:S(2)}) copy-start(f32[4,6,12,192]{3,0,2,1:T(4,128)} %param.3) | copy-start | bytes 663556
  252.5 4.4 %copy-start.1 = (f32[6,12,192]{2,1,0:T(8,128)S(1)}, f32[6,12,192]{2,1,0:T(8,128)}, u32[]{:S(2)}) copy-start(f32[6,12,192]{2,1,0:T(8,128)} %param.4) | copy-start | bytes 165892
